TPU v7x, 32 devices: a whole 2x2x4 slice. The times are simulated.
32 devices in a mesh: section: 4 (over y, x), dom: 8 (over z, core).
Axes of the slice: x: 2, y: 2, z: 4, core: 2. Of those that a mesh axis runs over, the one named last changes fastest.
Arguments:
- stacked: bfloat16 [4, 1024, 1024], P('section', 'dom'), may hold values from -6 to 6
- edges: int32 [1024, 256], P('dom'), may hold values 0 or 1
- picks: int32 [16, 3], P('dom'), may hold values from 0 to 2
- self_w: bfloat16 [4, 1024, 1024], P('section'), may hold values from -0.1875 to 0.1875
- neigh_w: bfloat16 [4, 1024, 1024], P('section'), may hold values from -0.75 to 0.75
Outputs:
- embeddings: bfloat16 [4, 1024, 1024], P('section', 'dom')
Inputs may be any that keep to these rules, and one draw needn't show every extreme that they name: `picks`: A value of 2 means that the destination block has no tile from that direction; smaller values name a slab of the peer partition.
All inputs are finite; a program needn't handle non-finite values. No bound on the sum of `edges` on one device may be relied on, other than what follows from the above.
Results may differ from a plain program's by a relative error of at most 0.006.
Values may be sent and summed in bfloat16 or wider, within the bound.
A program may use at most 64 MiB of HBM per device.

v0:
```python
import jax
import jax.numpy as jnp
from jax import lax
from jax.sharding import PartitionSpec as P

BLOCK = 64


peer_offsets = (-1, 1, 2)


def passed_along(block, axis, distance):
    devices = range(lax.axis_size(axis))
    route = [((i - distance) % len(devices), i) for i in devices]
    return lax.ppermute(block, axis, route)


def from_behind(value, axis, steps):
    count = lax.axis_size(axis)
    initial, last = (max(0, -steps), min(count, count - steps))
    return lax.ppermute(value, axis, [(source, source + steps) for source in range(initial, last)])


def tile_term(edge_rows, position, source_rows):
    tile_mask = edge_rows[:, position * BLOCK : (position + 1) * BLOCK]
    product = jnp.dot(
        tile_mask.astype(jnp.bfloat16), source_rows, preferred_element_type=jnp.float32
    )
    return (product, jnp.sum(tile_mask.astype(jnp.float32), axis=1))


def per_device(stacked, edges, picks, self_w, neigh_w):
    node_rows = stacked.shape[1]
    feature_width = stacked.shape[2]
    slab_count = node_rows // BLOCK
    section_index = lax.axis_index("section")
    weight_self = self_w[0]
    weight_neigh = neigh_w[0]
    asked = []
    for position in range(3):
        asked.append(passed_along(picks[:, position], "dom", peer_offsets[position]))

    def chosen(buffer, position, slab_now):
        wanted = lax.dynamic_index_in_dim(asked[position], slab_now, 0, keepdims=False)
        wanted = jnp.minimum(wanted, slab_count - 1)
        return lax.dynamic_slice_in_dim(buffer, wanted * BLOCK, BLOCK, 0)

    def fetch(buffer, slab_now):
        lower = passed_along(chosen(buffer, 0, slab_now), "dom", 1)
        uppers = []
        for position in (1, 2):
            uppers.append(
                passed_along(chosen(buffer, position, slab_now), "dom", -peer_offsets[position])
            )
        return (lower, uppers[0], uppers[1])

    def one_step(step_now, carry):
        buffer, result, incoming = carry
        slab_raw = step_now - section_index
        active = (slab_raw >= 0) & (slab_raw < slab_count)
        slab_now = jnp.clip(slab_raw, 0, slab_count - 1)
        refresh = active & (section_index > 0)
        start_row = slab_now * BLOCK
        current = lax.dynamic_slice_in_dim(buffer, start_row, BLOCK, 0)
        own_rows = jnp.where(refresh, incoming, current)
        buffer = lax.dynamic_update_slice_in_dim(buffer, own_rows, start_row, 0)
        edge_rows = lax.dynamic_slice_in_dim(edges, start_row, BLOCK, 0)
        live_row = lax.dynamic_index_in_dim(picks, slab_now, 0, keepdims=False) < slab_count
        received = fetch(buffer, slab_now)
        local_sum, local_count = tile_term(edge_rows, 0, own_rows)
        self_part = jnp.dot(own_rows, weight_self, preferred_element_type=jnp.float32)
        summed = local_sum
        degree = 1.0 + local_count
        for position in range(3):
            term, counted = tile_term(edge_rows, position + 1, received[position])
            summed = summed + jnp.where(live_row[position], term, 0.0)
            degree = degree + jnp.where(live_row[position], counted, 0.0)
        mean_rows = (summed / degree[:, None]).astype(jnp.bfloat16)
        hidden = self_part + jnp.dot(mean_rows, weight_neigh, preferred_element_type=jnp.float32)
        produced = jnp.maximum(hidden, 0.0).astype(jnp.bfloat16)
        previous = lax.dynamic_slice_in_dim(result, start_row, BLOCK, 0)
        result = lax.dynamic_update_slice_in_dim(
            result, jnp.where(active, produced, previous), start_row, 0
        )
        incoming = from_behind(produced, "section", 1)
        return (buffer, result, incoming)

    initial = (
        stacked[0],
        jnp.zeros_like(stacked[0]),
        jnp.zeros((BLOCK, feature_width), jnp.bfloat16),
    )
    final = lax.fori_loop(0, slab_count + lax.axis_size("section") - 1, one_step, initial)
    return final[1][None]


def solution(mesh):
    in_specs = (
        P("section", "dom", None),
        P("dom", None),
        P("dom", None),
        P("section", None, None),
        P("section", None, None),
    )
    out_specs = P("section", "dom", None)
    return jax.shard_map(
        per_device, mesh=mesh, in_specs=in_specs, out_specs=out_specs, check_vma=False
    )
```

profile of v0, /device:TPU:4, one launch (start us, length us, event | category | flops | bytes accessed | tf_op | source)
XLA Modules:
  0.0 151.2 jit_solution(4879521103698347559)
XLA Ops:
  2.0 3.1 %collective-permute-start.4 = (s32[2]{0:T(128)S(1)}, s32[2]{0:T(128)S(1)}, u32[]{:S(2)}, u32[]{:S(2)}) collective-permute-start(s32[2]{0:T(128)S(1)} %get-tuple-element.264), channel_id=1, source_target_pairs={{1,0},{2,1},{3,2},{4,3},{5,4},{6,5},{7,6},{0,7},{9,8},{10,9},{11,1... | collective-permute-start | bytes 32 | tf_op jit(solution)/shard_map/ppermute | solution.py:15
  6.3 3.5 %collective-permute-done.5 = s32[2]{0:T(128)S(1)} collective-permute-done((s32[2]{0:T(128)S(1)}, s32[2]{0:T(128)S(1)}, u32[]{:S(2)}, u32[]{:S(2)}) %collective-permute-start.5) | collective-permute-done | bytes 40 | tf_op jit(solution)/shard_map/ppermute | solution.py:15
  11.2 140.0 %while.18 = (s32[]{:T(128)}, bf16[128,1024]{1,0:T(8,128)(2,1)S(1)}, bf16[128,1024]{1,0:T(8,128)(2,1)}, bf16[64,1024]{1,0:T(8,128)(2,1)S(1)}, s32[]{:T(128)}, /*i...) while((s32[]{:T(128)}, bf16[128,1024]{1,0:T(8,128)(2,1)S(1)}, ...), condition=%wide.region_5.6_spmd, body=%wide.region_0.5_spmd.sunk | while | flops 302891200 | bytes 19863640 | solution.py:93
  15.2 3.5 %collective-permute-start.1 = (bf16[64,1024]{1,0:T(8,128)(2,1)S(1)}, bf16[64,1024]{1,0:T(8,128)(2,1)S(1)}, u32[]{:S(2)}, u32[]{:S(2)}) collective-permute-start(bf16[64,1024]{1,0:T(8,128)(2,1)S(1)} %get-tuple-element.398), channel_id=1, source_target_pairs={{1,0},{2,1},{3,2},{4,3},{5,4},{6,5},{7,6},{0,7},{9,8},{10,9},{11,1... | collective-permute-start | bytes 393224 | tf_op jit(solution)/shard_map/while/body/eval_jaxpr/ppermute | solution.py:15
  21.0 2.2 %fusion.47 = f32[64,1024]{1,0:T(8,128)S(1)} fusion(bf16[64,1024]{1,0:T(8,128)(2,1)S(1)} %get-tuple-element.395, bf16[1024,1024]{1,0:T(8,128)(2,1)} %get-tuple-element.460), kind=kOutput, calls=%fused_computation.43.clone.1 | convolution fusion | flops 134217728 | bytes 2490368 | tf_op jit(solution)/shard_map/while/body/eval_jaxpr/dot_general | solution.py:71
  23.5 1.9 %fusion.53 = f32[64]{0:T(128)S(1)} fusion(f32[64]{0:T(128)S(1)} %get-tuple-element.401, pred[]{:T(512)} %bitcast.40, f32[64]{0:T(128)S(1)} %get-tuple-element.402, pred[]{:T(512)} %bitcast.41, f32[64]{0:T(128)S(1)} %get-tuple-element.403, pred[]{:T(512)} %bitcast.42, f32[64]{0:T(128)S(1)} %get-tuple-element.405), kind=kLoop, calls=%fused_computation.36.clone.1 | loop fusion | flops 448 | bytes 1283 | tf_op jit(solution)/shard_map/while/body/eval_jaxpr/add | solution.py:77
  28.0 2.9 %select_dynamic-update-slice_fusion.2 = (bf16[128,1024]{1,0:T(8,128)(2,1)}, bf16[64,1024]{1,0:T(8,128)(2,1)S(1)}) fusion(bf16[128,1024]{1,0:T(8,128)(2,1)} %get-tuple-element.433, s32[]{:T(128)S(6)} %select_n.272, pred[]{:T(512)S(6)} %and.19, f32[64,1024]{1,0:T(8,128)S(1)} %fusion.47, bf16[1024,1024]{1,0:T(8,128)(2,1)S(1)} %copy-done, ...), kind=kOutput, calls=%fused_computation.11.clone.1 | convolution fusion | flops 143134720 | bytes 3181568 | tf_op jit(solution)/shard_map/while/body/eval_jaxpr/dot_general | solution.py:79
  30.9 3.4 %collective-permute-start.3 = (bf16[64,1024]{1,0:T(8,128)(2,1)S(1)}, bf16[64,1024]{1,0:T(8,128)(2,1)S(1)}, u32[]{:S(2)}, u32[]{:S(2)}) collective-permute-start(bf16[64,1024]{1,0:T(8,128)(2,1)S(1)} %get-tuple-element.407), channel_id=1, source_target_pairs={{0,8},{8,16},{16,24},{1,9},{9,17},{17,25},{2,10},{10,18},{18,26},{... | collective-permute-start | bytes 393224 | tf_op jit(solution)/shard_map/while/body/eval_jaxpr/ppermute | solution.py:21
  34.3 4.9 %collective-permute-done.3 = bf16[64,1024]{1,0:T(8,128)(2,1)S(1)} collective-permute-done((bf16[64,1024]{1,0:T(8,128)(2,1)S(1)}, bf16[64,1024]{1,0:T(8,128)(2,1)S(1)}, u32[]{:S(2)}, u32[]{:S(2)}) %collective-permute-start.3) | collective-permute-done | bytes 131104 | tf_op jit(solution)/shard_map/while/body/eval_jaxpr/ppermute | solution.py:21
  43.2 3.5 %collective-permute-start.1 = (bf16[64,1024]{1,0:T(8,128)(2,1)S(1)}, bf16[64,1024]{1,0:T(8,128)(2,1)S(1)}, u32[]{:S(2)}, u32[]{:S(2)}) collective-permute-start(bf16[64,1024]{1,0:T(8,128)(2,1)S(1)} %get-tuple-element.398), channel_id=1, source_target_pairs={{1,0},{2,1},{3,2},{4,3},{5,4},{6,5},{7,6},{0,7},{9,8},{10,9},{11,1... | collective-permute-start | bytes 393224 | tf_op jit(solution)/shard_map/while/body/eval_jaxpr/ppermute | solution.py:15
  49.0 2.2 %fusion.47 = f32[64,1024]{1,0:T(8,128)S(1)} fusion(bf16[64,1024]{1,0:T(8,128)(2,1)S(1)} %get-tuple-element.395, bf16[1024,1024]{1,0:T(8,128)(2,1)} %get-tuple-element.460), kind=kOutput, calls=%fused_computation.43.clone.1 | convolution fusion | flops 134217728 | bytes 2490368 | tf_op jit(solution)/shard_map/while/body/eval_jaxpr/dot_general | solution.py:71
  51.5 1.9 %fusion.53 = f32[64]{0:T(128)S(1)} fusion(f32[64]{0:T(128)S(1)} %get-tuple-element.401, pred[]{:T(512)} %bitcast.40, f32[64]{0:T(128)S(1)} %get-tuple-element.402, pred[]{:T(512)} %bitcast.41, f32[64]{0:T(128)S(1)} %get-tuple-element.403, pred[]{:T(512)} %bitcast.42, f32[64]{0:T(128)S(1)} %get-tuple-element.405), kind=kLoop, calls=%fused_computation.36.clone.1 | loop fusion | flops 448 | bytes 1283 | tf_op jit(solution)/shard_map/while/body/eval_jaxpr/add | solution.py:77
  56.0 2.9 %select_dynamic-update-slice_fusion.2 = (bf16[128,1024]{1,0:T(8,128)(2,1)}, bf16[64,1024]{1,0:T(8,128)(2,1)S(1)}) fusion(bf16[128,1024]{1,0:T(8,128)(2,1)} %get-tuple-element.433, s32[]{:T(128)S(6)} %select_n.272, pred[]{:T(512)S(6)} %and.19, f32[64,1024]{1,0:T(8,128)S(1)} %fusion.47, bf16[1024,1024]{1,0:T(8,128)(2,1)S(1)} %copy-done, ...), kind=kOutput, calls=%fused_computation.11.clone.1 | convolution fusion | flops 143134720 | bytes 3181568 | tf_op jit(solution)/shard_map/while/body/eval_jaxpr/dot_general | solution.py:79
  58.9 2.5 %collective-permute-start.3 = (bf16[64,1024]{1,0:T(8,128)(2,1)S(1)}, bf16[64,1024]{1,0:T(8,128)(2,1)S(1)}, u32[]{:S(2)}, u32[]{:S(2)}) collective-permute-start(bf16[64,1024]{1,0:T(8,128)(2,1)S(1)} %get-tuple-element.407), channel_id=1, source_target_pairs={{0,8},{8,16},{16,24},{1,9},{9,17},{17,25},{2,10},{10,18},{18,26},{... | collective-permute-start | bytes 393224 | tf_op jit(solution)/shard_map/while/body/eval_jaxpr/ppermute | solution.py:21
  61.4 5.8 %collective-permute-done.3 = bf16[64,1024]{1,0:T(8,128)(2,1)S(1)} collective-permute-done((bf16[64,1024]{1,0:T(8,128)(2,1)S(1)}, bf16[64,1024]{1,0:T(8,128)(2,1)S(1)}, u32[]{:S(2)}, u32[]{:S(2)}) %collective-permute-start.3) | collective-permute-done | bytes 131104 | tf_op jit(solution)/shard_map/while/body/eval_jaxpr/ppermute | solution.py:21
  71.2 3.5 %collective-permute-start.1 = (bf16[64,1024]{1,0:T(8,128)(2,1)S(1)}, bf16[64,1024]{1,0:T(8,128)(2,1)S(1)}, u32[]{:S(2)}, u32[]{:S(2)}) collective-permute-start(bf16[64,1024]{1,0:T(8,128)(2,1)S(1)} %get-tuple-element.398), channel_id=1, source_target_pairs={{1,0},{2,1},{3,2},{4,3},{5,4},{6,5},{7,6},{0,7},{9,8},{10,9},{11,1... | collective-permute-start | bytes 393224 | tf_op jit(solution)/shard_map/while/body/eval_jaxpr/ppermute | solution.py:15
  77.0 2.2 %fusion.47 = f32[64,1024]{1,0:T(8,128)S(1)} fusion(bf16[64,1024]{1,0:T(8,128)(2,1)S(1)} %get-tuple-element.395, bf16[1024,1024]{1,0:T(8,128)(2,1)} %get-tuple-element.460), kind=kOutput, calls=%fused_computation.43.clone.1 | convolution fusion | flops 134217728 | bytes 2490368 | tf_op jit(solution)/shard_map/while/body/eval_jaxpr/dot_general | solution.py:71
  79.5 1.9 %fusion.53 = f32[64]{0:T(128)S(1)} fusion(f32[64]{0:T(128)S(1)} %get-tuple-element.401, pred[]{:T(512)} %bitcast.40, f32[64]{0:T(128)S(1)} %get-tuple-element.402, pred[]{:T(512)} %bitcast.41, f32[64]{0:T(128)S(1)} %get-tuple-element.403, pred[]{:T(512)} %bitcast.42, f32[64]{0:T(128)S(1)} %get-tuple-element.405), kind=kLoop, calls=%fused_computation.36.clone.1 | loop fusion | flops 448 | bytes 1283 | tf_op jit(solution)/shard_map/while/body/eval_jaxpr/add | solution.py:77
  84.0 2.9 %select_dynamic-update-slice_fusion.2 = (bf16[128,1024]{1,0:T(8,128)(2,1)}, bf16[64,1024]{1,0:T(8,128)(2,1)S(1)}) fusion(bf16[128,1024]{1,0:T(8,128)(2,1)} %get-tuple-element.433, s32[]{:T(128)S(6)} %select_n.272, pred[]{:T(512)S(6)} %and.19, f32[64,1024]{1,0:T(8,128)S(1)} %fusion.47, bf16[1024,1024]{1,0:T(8,128)(2,1)S(1)} %copy-done, ...), kind=kOutput, calls=%fused_computation.11.clone.1 | convolution fusion | flops 143134720 | bytes 3181568 | tf_op jit(solution)/shard_map/while/body/eval_jaxpr/dot_general | solution.py:79
  86.9 1.9 %collective-permute-start.3 = (bf16[64,1024]{1,0:T(8,128)(2,1)S(1)}, bf16[64,1024]{1,0:T(8,128)(2,1)S(1)}, u32[]{:S(2)}, u32[]{:S(2)}) collective-permute-start(bf16[64,1024]{1,0:T(8,128)(2,1)S(1)} %get-tuple-element.407), channel_id=1, source_target_pairs={{0,8},{8,16},{16,24},{1,9},{9,17},{17,25},{2,10},{10,18},{18,26},{... | collective-permute-start | bytes 393224 | tf_op jit(solution)/shard_map/while/body/eval_jaxpr/ppermute | solution.py:21
  88.8 6.4 %collective-permute-done.3 = bf16[64,1024]{1,0:T(8,128)(2,1)S(1)} collective-permute-done((bf16[64,1024]{1,0:T(8,128)(2,1)S(1)}, bf16[64,1024]{1,0:T(8,128)(2,1)S(1)}, u32[]{:S(2)}, u32[]{:S(2)}) %collective-permute-start.3) | collective-permute-done | bytes 131104 | tf_op jit(solution)/shard_map/while/body/eval_jaxpr/ppermute | solution.py:21
  99.2 3.5 %collective-permute-start.1 = (bf16[64,1024]{1,0:T(8,128)(2,1)S(1)}, bf16[64,1024]{1,0:T(8,128)(2,1)S(1)}, u32[]{:S(2)}, u32[]{:S(2)}) collective-permute-start(bf16[64,1024]{1,0:T(8,128)(2,1)S(1)} %get-tuple-element.398), channel_id=1, source_target_pairs={{1,0},{2,1},{3,2},{4,3},{5,4},{6,5},{7,6},{0,7},{9,8},{10,9},{11,1... | collective-permute-start | bytes 393224 | tf_op jit(solution)/shard_map/while/body/eval_jaxpr/ppermute | solution.py:15
  105.0 2.2 %fusion.47 = f32[64,1024]{1,0:T(8,128)S(1)} fusion(bf16[64,1024]{1,0:T(8,128)(2,1)S(1)} %get-tuple-element.395, bf16[1024,1024]{1,0:T(8,128)(2,1)} %get-tuple-element.460), kind=kOutput, calls=%fused_computation.43.clone.1 | convolution fusion | flops 134217728 | bytes 2490368 | tf_op jit(solution)/shard_map/while/body/eval_jaxpr/dot_general | solution.py:71
  107.5 1.9 %fusion.53 = f32[64]{0:T(128)S(1)} fusion(f32[64]{0:T(128)S(1)} %get-tuple-element.401, pred[]{:T(512)} %bitcast.40, f32[64]{0:T(128)S(1)} %get-tuple-element.402, pred[]{:T(512)} %bitcast.41, f32[64]{0:T(128)S(1)} %get-tuple-element.403, pred[]{:T(512)} %bitcast.42, f32[64]{0:T(128)S(1)} %get-tuple-element.405), kind=kLoop, calls=%fused_computation.36.clone.1 | loop fusion | flops 448 | bytes 1283 | tf_op jit(solution)/shard_map/while/body/eval_jaxpr/add | solution.py:77
  112.0 2.9 %select_dynamic-update-slice_fusion.2 = (bf16[128,1024]{1,0:T(8,128)(2,1)}, bf16[64,1024]{1,0:T(8,128)(2,1)S(1)}) fusion(bf16[128,1024]{1,0:T(8,128)(2,1)} %get-tuple-element.433, s32[]{:T(128)S(6)} %select_n.272, pred[]{:T(512)S(6)} %and.19, f32[64,1024]{1,0:T(8,128)S(1)} %fusion.47, bf16[1024,1024]{1,0:T(8,128)(2,1)S(1)} %copy-done, ...), kind=kOutput, calls=%fused_computation.11.clone.1 | convolution fusion | flops 143134720 | bytes 3181568 | tf_op jit(solution)/shard_map/while/body/eval_jaxpr/dot_general | solution.py:79
  114.9 1.9 %collective-permute-start.3 = (bf16[64,1024]{1,0:T(8,128)(2,1)S(1)}, bf16[64,1024]{1,0:T(8,128)(2,1)S(1)}, u32[]{:S(2)}, u32[]{:S(2)}) collective-permute-start(bf16[64,1024]{1,0:T(8,128)(2,1)S(1)} %get-tuple-element.407), channel_id=1, source_target_pairs={{0,8},{8,16},{16,24},{1,9},{9,17},{17,25},{2,10},{10,18},{18,26},{... | collective-permute-start | bytes 393224 | tf_op jit(solution)/shard_map/while/body/eval_jaxpr/ppermute | solution.py:21
  116.8 6.4 %collective-permute-done.3 = bf16[64,1024]{1,0:T(8,128)(2,1)S(1)} collective-permute-done((bf16[64,1024]{1,0:T(8,128)(2,1)S(1)}, bf16[64,1024]{1,0:T(8,128)(2,1)S(1)}, u32[]{:S(2)}, u32[]{:S(2)}) %collective-permute-start.3) | collective-permute-done | bytes 131104 | tf_op jit(solution)/shard_map/while/body/eval_jaxpr/ppermute | solution.py:21
  127.2 3.5 %collective-permute-start.1 = (bf16[64,1024]{1,0:T(8,128)(2,1)S(1)}, bf16[64,1024]{1,0:T(8,128)(2,1)S(1)}, u32[]{:S(2)}, u32[]{:S(2)}) collective-permute-start(bf16[64,1024]{1,0:T(8,128)(2,1)S(1)} %get-tuple-element.398), channel_id=1, source_target_pairs={{1,0},{2,1},{3,2},{4,3},{5,4},{6,5},{7,6},{0,7},{9,8},{10,9},{11,1... | collective-permute-start | bytes 393224 | tf_op jit(solution)/shard_map/while/body/eval_jaxpr/ppermute | solution.py:15
  133.0 2.2 %fusion.47 = f32[64,1024]{1,0:T(8,128)S(1)} fusion(bf16[64,1024]{1,0:T(8,128)(2,1)S(1)} %get-tuple-element.395, bf16[1024,1024]{1,0:T(8,128)(2,1)} %get-tuple-element.460), kind=kOutput, calls=%fused_computation.43.clone.1 | convolution fusion | flops 134217728 | bytes 2490368 | tf_op jit(solution)/shard_map/while/body/eval_jaxpr/dot_general | solution.py:71
  140.0 2.9 %select_dynamic-update-slice_fusion.2 = (bf16[128,1024]{1,0:T(8,128)(2,1)}, bf16[64,1024]{1,0:T(8,128)(2,1)S(1)}) fusion(bf16[128,1024]{1,0:T(8,128)(2,1)} %get-tuple-element.433, s32[]{:T(128)S(6)} %select_n.272, pred[]{:T(512)S(6)} %and.19, f32[64,1024]{1,0:T(8,128)S(1)} %fusion.47, bf16[1024,1024]{1,0:T(8,128)(2,1)S(1)} %copy-done, ...), kind=kOutput, calls=%fused_computation.11.clone.1 | convolution fusion | flops 143134720 | bytes 3181568 | tf_op jit(solution)/shard_map/while/body/eval_jaxpr/dot_general | solution.py:79
  142.9 1.9 %collective-permute-start.3 = (bf16[64,1024]{1,0:T(8,128)(2,1)S(1)}, bf16[64,1024]{1,0:T(8,128)(2,1)S(1)}, u32[]{:S(2)}, u32[]{:S(2)}) collective-permute-start(bf16[64,1024]{1,0:T(8,128)(2,1)S(1)} %get-tuple-element.407), channel_id=1, source_target_pairs={{0,8},{8,16},{16,24},{1,9},{9,17},{17,25},{2,10},{10,18},{18,26},{... | collective-permute-start | bytes 393224 | tf_op jit(solution)/shard_map/while/body/eval_jaxpr/ppermute | solution.py:21
  144.8 6.4 %collective-permute-done.3 = bf16[64,1024]{1,0:T(8,128)(2,1)S(1)} collective-permute-done((bf16[64,1024]{1,0:T(8,128)(2,1)S(1)}, bf16[64,1024]{1,0:T(8,128)(2,1)S(1)}, u32[]{:S(2)}, u32[]{:S(2)}) %collective-permute-start.3) | collective-permute-done | bytes 131104 | tf_op jit(solution)/shard_map/while/body/eval_jaxpr/ppermute | solution.py:21
  (109 shorter events, 42.1 us)
Async XLA Ops:
  2.0 4.4 %collective-permute-start.4 = (s32[2]{0:T(128)S(1)}, s32[2]{0:T(128)S(1)}, u32[]{:S(2)}, u32[]{:S(2)}) collective-permute-start(s32[2]{0:T(128)S(1)} %get-tuple-element.264), channel_id=1, source_target_pairs={{1,0},{2,1},{3,2},{4,3},{5,4},{6,5},{7,6},{0,7},{9,8},{10,9},{11,1... | collective-permute-start | bytes 32 | tf_op jit(solution)/shard_map/ppermute | solution.py:15
  5.0 4.8 %collective-permute-start.5 = (s32[2]{0:T(128)S(1)}, s32[2]{0:T(128)S(1)}, u32[]{:S(2)}, u32[]{:S(2)}) collective-permute-start(s32[2]{0:T(128)S(1)} %get-tuple-element.263), channel_id=1, source_target_pairs={{7,0},{0,1},{1,2},{2,3},{3,4},{4,5},{5,6},{6,7},{15,8},{8,9},{9,10... | collective-permute-start | bytes 32 | tf_op jit(solution)/shard_map/ppermute | solution.py:15
  5.1 5.4 %collective-permute-start.6 = (s32[2]{0:T(128)S(1)}, s32[2]{0:T(128)S(1)}, u32[]{:S(2)}, u32[]{:S(2)}) collective-permute-start(s32[2]{0:T(128)S(1)} %get-tuple-element.262), channel_id=1, source_target_pairs={{6,0},{7,1},{0,2},{1,3},{2,4},{3,5},{4,6},{5,7},{14,8},{15,9},{8,1... | collective-permute-start | bytes 32 | tf_op jit(solution)/shard_map/ppermute | solution.py:15
  15.0 8.2 %copy-start.1 = (s32[128,256]{1,0:T(8,128)S(1)}, s32[128,256]{1,0:T(8,128)}, u32[]{:S(2)}) copy-start(s32[128,256]{1,0:T(8,128)} %get-tuple-element.461) | copy-start | bytes 393220 | tf_op jit(solution)/shard_map/while
  15.1 10.2 %collective-permute-start = (bf16[64,1024]{1,0:T(8,128)(2,1)S(1)}, bf16[64,1024]{1,0:T(8,128)(2,1)}, u32[]{:S(2)}, u32[]{:S(2)}) collective-permute-start(bf16[64,1024]{1,0:T(8,128)(2,1)S(1)} %get-tuple-element.396), channel_id=1, source_target_pairs={{7,0},{0,1},{1,2},{2,3},{3,4},{4,5},{5,6},{6,7},{15,8},{8,9},{9,10... | collective-permute-start | bytes 393224 | tf_op jit(solution)/shard_map/while/body/eval_jaxpr/ppermute | solution.py:15
  15.2 12.0 %collective-permute-start.1 = (bf16[64,1024]{1,0:T(8,128)(2,1)S(1)}, bf16[64,1024]{1,0:T(8,128)(2,1)S(1)}, u32[]{:S(2)}, u32[]{:S(2)}) collective-permute-start(bf16[64,1024]{1,0:T(8,128)(2,1)S(1)} %get-tuple-element.398), channel_id=1, source_target_pairs={{1,0},{2,1},{3,2},{4,3},{5,4},{6,5},{7,6},{0,7},{9,8},{10,9},{11,1... | collective-permute-start | bytes 393224 | tf_op jit(solution)/shard_map/while/body/eval_jaxpr/ppermute | solution.py:15
  18.7 9.2 %collective-permute-start.2 = (bf16[64,1024]{1,0:T(8,128)(2,1)S(1)}, bf16[64,1024]{1,0:T(8,128)(2,1)S(1)}, u32[]{:S(2)}, u32[]{:S(2)}) collective-permute-start(bf16[64,1024]{1,0:T(8,128)(2,1)S(1)} %get-tuple-element.400), channel_id=1, source_target_pairs={{2,0},{3,1},{4,2},{5,3},{6,4},{7,5},{0,6},{1,7},{10,8},{11,9},{12,... | collective-permute-start | bytes 393224 | tf_op jit(solution)/shard_map/while/body/eval_jaxpr/ppermute | solution.py:15
  21.0 7.0 %copy-start = (bf16[1024,1024]{1,0:T(8,128)(2,1)S(1)}, bf16[1024,1024]{1,0:T(8,128)(2,1)}, u32[]{:S(2)}) copy-start(bf16[1024,1024]{1,0:T(8,128)(2,1)} %get-tuple-element.466) | copy-start | bytes 6291460 | tf_op jit(solution)/shard_map/while
  30.9 8.3 %collective-permute-start.3 = (bf16[64,1024]{1,0:T(8,128)(2,1)S(1)}, bf16[64,1024]{1,0:T(8,128)(2,1)S(1)}, u32[]{:S(2)}, u32[]{:S(2)}) collective-permute-start(bf16[64,1024]{1,0:T(8,128)(2,1)S(1)} %get-tuple-element.407), channel_id=1, source_target_pairs={{0,8},{8,16},{16,24},{1,9},{9,17},{17,25},{2,10},{10,18},{18,26},{... | collective-permute-start | bytes 393224 | tf_op jit(solution)/shard_map/while/body/eval_jaxpr/ppermute | solution.py:21
  43.0 8.2 %copy-start.1 = (s32[128,256]{1,0:T(8,128)S(1)}, s32[128,256]{1,0:T(8,128)}, u32[]{:S(2)}) copy-start(s32[128,256]{1,0:T(8,128)} %get-tuple-element.461) | copy-start | bytes 393220 | tf_op jit(solution)/shard_map/while
  43.1 10.2 %collective-permute-start = (bf16[64,1024]{1,0:T(8,128)(2,1)S(1)}, bf16[64,1024]{1,0:T(8,128)(2,1)}, u32[]{:S(2)}, u32[]{:S(2)}) collective-permute-start(bf16[64,1024]{1,0:T(8,128)(2,1)S(1)} %get-tuple-element.396), channel_id=1, source_target_pairs={{7,0},{0,1},{1,2},{2,3},{3,4},{4,5},{5,6},{6,7},{15,8},{8,9},{9,10... | collective-permute-start | bytes 393224 | tf_op jit(solution)/shard_map/while/body/eval_jaxpr/ppermute | solution.py:15
  43.2 12.0 %collective-permute-start.1 = (bf16[64,1024]{1,0:T(8,128)(2,1)S(1)}, bf16[64,1024]{1,0:T(8,128)(2,1)S(1)}, u32[]{:S(2)}, u32[]{:S(2)}) collective-permute-start(bf16[64,1024]{1,0:T(8,128)(2,1)S(1)} %get-tuple-element.398), channel_id=1, source_target_pairs={{1,0},{2,1},{3,2},{4,3},{5,4},{6,5},{7,6},{0,7},{9,8},{10,9},{11,1... | collective-permute-start | bytes 393224 | tf_op jit(solution)/shard_map/while/body/eval_jaxpr/ppermute | solution.py:15
  46.7 9.2 %collective-permute-start.2 = (bf16[64,1024]{1,0:T(8,128)(2,1)S(1)}, bf16[64,1024]{1,0:T(8,128)(2,1)S(1)}, u32[]{:S(2)}, u32[]{:S(2)}) collective-permute-start(bf16[64,1024]{1,0:T(8,128)(2,1)S(1)} %get-tuple-element.400), channel_id=1, source_target_pairs={{2,0},{3,1},{4,2},{5,3},{6,4},{7,5},{0,6},{1,7},{10,8},{11,9},{12,... | collective-permute-start | bytes 393224 | tf_op jit(solution)/shard_map/while/body/eval_jaxpr/ppermute | solution.py:15
  49.0 7.0 %copy-start = (bf16[1024,1024]{1,0:T(8,128)(2,1)S(1)}, bf16[1024,1024]{1,0:T(8,128)(2,1)}, u32[]{:S(2)}) copy-start(bf16[1024,1024]{1,0:T(8,128)(2,1)} %get-tuple-element.466) | copy-start | bytes 6291460 | tf_op jit(solution)/shard_map/while
  58.9 8.3 %collective-permute-start.3 = (bf16[64,1024]{1,0:T(8,128)(2,1)S(1)}, bf16[64,1024]{1,0:T(8,128)(2,1)S(1)}, u32[]{:S(2)}, u32[]{:S(2)}) collective-permute-start(bf16[64,1024]{1,0:T(8,128)(2,1)S(1)} %get-tuple-element.407), channel_id=1, source_target_pairs={{0,8},{8,16},{16,24},{1,9},{9,17},{17,25},{2,10},{10,18},{18,26},{... | collective-permute-start | bytes 393224 | tf_op jit(solution)/shard_map/while/body/eval_jaxpr/ppermute | solution.py:21
  71.0 8.2 %copy-start.1 = (s32[128,256]{1,0:T(8,128)S(1)}, s32[128,256]{1,0:T(8,128)}, u32[]{:S(2)}) copy-start(s32[128,256]{1,0:T(8,128)} %get-tuple-element.461) | copy-start | bytes 393220 | tf_op jit(solution)/shard_map/while
  71.1 10.2 %collective-permute-start = (bf16[64,1024]{1,0:T(8,128)(2,1)S(1)}, bf16[64,1024]{1,0:T(8,128)(2,1)}, u32[]{:S(2)}, u32[]{:S(2)}) collective-permute-start(bf16[64,1024]{1,0:T(8,128)(2,1)S(1)} %get-tuple-element.396), channel_id=1, source_target_pairs={{7,0},{0,1},{1,2},{2,3},{3,4},{4,5},{5,6},{6,7},{15,8},{8,9},{9,10... | collective-permute-start | bytes 393224 | tf_op jit(solution)/shard_map/while/body/eval_jaxpr/ppermute | solution.py:15
  71.2 12.0 %collective-permute-start.1 = (bf16[64,1024]{1,0:T(8,128)(2,1)S(1)}, bf16[64,1024]{1,0:T(8,128)(2,1)S(1)}, u32[]{:S(2)}, u32[]{:S(2)}) collective-permute-start(bf16[64,1024]{1,0:T(8,128)(2,1)S(1)} %get-tuple-element.398), channel_id=1, source_target_pairs={{1,0},{2,1},{3,2},{4,3},{5,4},{6,5},{7,6},{0,7},{9,8},{10,9},{11,1... | collective-permute-start | bytes 393224 | tf_op jit(solution)/shard_map/while/body/eval_jaxpr/ppermute | solution.py:15
  74.7 9.2 %collective-permute-start.2 = (bf16[64,1024]{1,0:T(8,128)(2,1)S(1)}, bf16[64,1024]{1,0:T(8,128)(2,1)S(1)}, u32[]{:S(2)}, u32[]{:S(2)}) collective-permute-start(bf16[64,1024]{1,0:T(8,128)(2,1)S(1)} %get-tuple-element.400), channel_id=1, source_target_pairs={{2,0},{3,1},{4,2},{5,3},{6,4},{7,5},{0,6},{1,7},{10,8},{11,9},{12,... | collective-permute-start | bytes 393224 | tf_op jit(solution)/shard_map/while/body/eval_jaxpr/ppermute | solution.py:15
  86.9 8.3 %collective-permute-start.3 = (bf16[64,1024]{1,0:T(8,128)(2,1)S(1)}, bf16[64,1024]{1,0:T(8,128)(2,1)S(1)}, u32[]{:S(2)}, u32[]{:S(2)}) collective-permute-start(bf16[64,1024]{1,0:T(8,128)(2,1)S(1)} %get-tuple-element.407), channel_id=1, source_target_pairs={{0,8},{8,16},{16,24},{1,9},{9,17},{17,25},{2,10},{10,18},{18,26},{... | collective-permute-start | bytes 393224 | tf_op jit(solution)/shard_map/while/body/eval_jaxpr/ppermute | solution.py:21
  99.0 8.2 %copy-start.1 = (s32[128,256]{1,0:T(8,128)S(1)}, s32[128,256]{1,0:T(8,128)}, u32[]{:S(2)}) copy-start(s32[128,256]{1,0:T(8,128)} %get-tuple-element.461) | copy-start | bytes 393220 | tf_op jit(solution)/shard_map/while
  99.1 10.2 %collective-permute-start = (bf16[64,1024]{1,0:T(8,128)(2,1)S(1)}, bf16[64,1024]{1,0:T(8,128)(2,1)}, u32[]{:S(2)}, u32[]{:S(2)}) collective-permute-start(bf16[64,1024]{1,0:T(8,128)(2,1)S(1)} %get-tuple-element.396), channel_id=1, source_target_pairs={{7,0},{0,1},{1,2},{2,3},{3,4},{4,5},{5,6},{6,7},{15,8},{8,9},{9,10... | collective-permute-start | bytes 393224 | tf_op jit(solution)/shard_map/while/body/eval_jaxpr/ppermute | solution.py:15
  99.2 12.0 %collective-permute-start.1 = (bf16[64,1024]{1,0:T(8,128)(2,1)S(1)}, bf16[64,1024]{1,0:T(8,128)(2,1)S(1)}, u32[]{:S(2)}, u32[]{:S(2)}) collective-permute-start(bf16[64,1024]{1,0:T(8,128)(2,1)S(1)} %get-tuple-element.398), channel_id=1, source_target_pairs={{1,0},{2,1},{3,2},{4,3},{5,4},{6,5},{7,6},{0,7},{9,8},{10,9},{11,1... | collective-permute-start | bytes 393224 | tf_op jit(solution)/shard_map/while/body/eval_jaxpr/ppermute | solution.py:15
  102.7 9.2 %collective-permute-start.2 = (bf16[64,1024]{1,0:T(8,128)(2,1)S(1)}, bf16[64,1024]{1,0:T(8,128)(2,1)S(1)}, u32[]{:S(2)}, u32[]{:S(2)}) collective-permute-start(bf16[64,1024]{1,0:T(8,128)(2,1)S(1)} %get-tuple-element.400), channel_id=1, source_target_pairs={{2,0},{3,1},{4,2},{5,3},{6,4},{7,5},{0,6},{1,7},{10,8},{11,9},{12,... | collective-permute-start | bytes 393224 | tf_op jit(solution)/shard_map/while/body/eval_jaxpr/ppermute | solution.py:15
  105.0 7.0 %copy-start = (bf16[1024,1024]{1,0:T(8,128)(2,1)S(1)}, bf16[1024,1024]{1,0:T(8,128)(2,1)}, u32[]{:S(2)}) copy-start(bf16[1024,1024]{1,0:T(8,128)(2,1)} %get-tuple-element.466) | copy-start | bytes 6291460 | tf_op jit(solution)/shard_map/while
  114.9 8.3 %collective-permute-start.3 = (bf16[64,1024]{1,0:T(8,128)(2,1)S(1)}, bf16[64,1024]{1,0:T(8,128)(2,1)S(1)}, u32[]{:S(2)}, u32[]{:S(2)}) collective-permute-start(bf16[64,1024]{1,0:T(8,128)(2,1)S(1)} %get-tuple-element.407), channel_id=1, source_target_pairs={{0,8},{8,16},{16,24},{1,9},{9,17},{17,25},{2,10},{10,18},{18,26},{... | collective-permute-start | bytes 393224 | tf_op jit(solution)/shard_map/while/body/eval_jaxpr/ppermute | solution.py:21
  127.0 8.2 %copy-start.1 = (s32[128,256]{1,0:T(8,128)S(1)}, s32[128,256]{1,0:T(8,128)}, u32[]{:S(2)}) copy-start(s32[128,256]{1,0:T(8,128)} %get-tuple-element.461) | copy-start | bytes 393220 | tf_op jit(solution)/shard_map/while
  127.1 10.2 %collective-permute-start = (bf16[64,1024]{1,0:T(8,128)(2,1)S(1)}, bf16[64,1024]{1,0:T(8,128)(2,1)}, u32[]{:S(2)}, u32[]{:S(2)}) collective-permute-start(bf16[64,1024]{1,0:T(8,128)(2,1)S(1)} %get-tuple-element.396), channel_id=1, source_target_pairs={{7,0},{0,1},{1,2},{2,3},{3,4},{4,5},{5,6},{6,7},{15,8},{8,9},{9,10... | collective-permute-start | bytes 393224 | tf_op jit(solution)/shard_map/while/body/eval_jaxpr/ppermute | solution.py:15
  127.2 12.0 %collective-permute-start.1 = (bf16[64,1024]{1,0:T(8,128)(2,1)S(1)}, bf16[64,1024]{1,0:T(8,128)(2,1)S(1)}, u32[]{:S(2)}, u32[]{:S(2)}) collective-permute-start(bf16[64,1024]{1,0:T(8,128)(2,1)S(1)} %get-tuple-element.398), channel_id=1, source_target_pairs={{1,0},{2,1},{3,2},{4,3},{5,4},{6,5},{7,6},{0,7},{9,8},{10,9},{11,1... | collective-permute-start | bytes 393224 | tf_op jit(solution)/shard_map/while/body/eval_jaxpr/ppermute | solution.py:15
  130.7 9.2 %collective-permute-start.2 = (bf16[64,1024]{1,0:T(8,128)(2,1)S(1)}, bf16[64,1024]{1,0:T(8,128)(2,1)S(1)}, u32[]{:S(2)}, u32[]{:S(2)}) collective-permute-start(bf16[64,1024]{1,0:T(8,128)(2,1)S(1)} %get-tuple-element.400), channel_id=1, source_target_pairs={{2,0},{3,1},{4,2},{5,3},{6,4},{7,5},{0,6},{1,7},{10,8},{11,9},{12,... | collective-permute-start | bytes 393224 | tf_op jit(solution)/shard_map/while/body/eval_jaxpr/ppermute | solution.py:15
  133.0 7.0 %copy-start = (bf16[1024,1024]{1,0:T(8,128)(2,1)S(1)}, bf16[1024,1024]{1,0:T(8,128)(2,1)}, u32[]{:S(2)}) copy-start(bf16[1024,1024]{1,0:T(8,128)(2,1)} %get-tuple-element.466) | copy-start | bytes 6291460 | tf_op jit(solution)/shard_map/while
  142.9 8.3 %collective-permute-start.3 = (bf16[64,1024]{1,0:T(8,128)(2,1)S(1)}, bf16[64,1024]{1,0:T(8,128)(2,1)S(1)}, u32[]{:S(2)}, u32[]{:S(2)}) collective-permute-start(bf16[64,1024]{1,0:T(8,128)(2,1)S(1)} %get-tuple-element.407), channel_id=1, source_target_pairs={{0,8},{8,16},{16,24},{1,9},{9,17},{17,25},{2,10},{10,18},{18,26},{... | collective-permute-start | bytes 393224 | tf_op jit(solution)/shard_map/while/body/eval_jaxpr/ppermute | solution.py:21
  (1 other events, 7.0 us)
where the time goes:
time: 152 us; the launch traced here: 151 us
  matrix products  42.8 us (28%)
  waiting for transfers between devices  35.2 us (23%)
  starting transfers between devices  32.7 us (22%)
  local copies, waits for them, and re-layouts  15.8 us (10%)
  other arithmetic  14.3 us (9%)
  loops' own time  10.4 us (7%)
    ppermute x5, waiting for transfers between devices, from_behind(): lax.ppermute(value, axis, [(source, source + steps) for source in range(i...  29.8 us
    ppermute x18, starting transfers between devices, passed_along(): return lax.ppermute(block, axis, route)  21.1 us
    dot_general x15, matrix products, tile_term(): jnp.dot(tile_mask.astype(jnp.bfloat16), source_rows, preferred_element_ty...  17.4 us
    dot_general x5, matrix products, one_step(): jnp.dot(mean_rows, weight_neigh, preferred_element_type=jnp.float32)  14.4 us
    ppermute x5, starting transfers between devices, from_behind(): lax.ppermute(value, axis, [(source, source + steps) for source in range(i...  11.6 us
    dot_general x5, matrix products, one_step(): jnp.dot(own_rows, weight_self, preferred_element_type=jnp.float32)  11.1 us
    another operation x1, loops' own time, per_device(): lax.fori_loop(0, slab_count + lax.axis_size('section') - 1, one_step, ini...  10.4 us
    dynamic_slice x15, local copies, waits for them, and re-layouts, chosen(): lax.dynamic_index_in_dim(asked[position], slab_now, 0, keepdims=False)  9.56 us
  transfers between devices with their start and end apart: 23, of which 8 were waited for; matrix products, arithmetic and copies ran while one was open for 30% of the time, Pallas kernels for 0%

commit v1 on v0

v1 whole, which is shorter than its diff:
```python
import functools

import jax
import jax.numpy as jnp
from jax import lax
from jax.experimental import pallas as pl
from jax.experimental.pallas import tpu as pltpu
from jax.sharding import PartitionSpec as P

PEER_OFFSETS = (-1, 1, 2)
MESH = pl.DeviceIdType.MESH


def kernel(
    ns, nd, slabs, nch,
    stacked, edges, picks, ws_hbm, wn_hbm, out,
    ws, wn, src, masks, pre, acc, stage,
    wsem, zsend, zrecv, xsend, xrecv,
):
    block = edges.shape[1] // (len(PEER_OFFSETS) + 1)
    width = stacked.shape[1]
    cw = width // nch
    s = lax.axis_index("section")
    p = lax.axis_index("dom")

    def at(section, dom):
        return {"section": section, "dom": dom}

    w_self = pltpu.make_async_copy(ws_hbm, ws, wsem.at[0])
    w_neigh = pltpu.make_async_copy(wn_hbm, wn, wsem.at[1])
    w_self.start()
    w_neigh.start()

    barrier = pltpu.get_barrier_semaphore()
    greeted = [at(s, lax.rem(p + o + nd, nd)) for o in (-2, -1, 1, 2)]
    greeted += [at(lax.rem(s + 1, ns), p), at(lax.rem(s + ns - 1, ns), p)]
    for device in greeted:
        pl.semaphore_signal(barrier, inc=1, device_id=device, device_id_type=MESH)

    def rows(c):
        return pl.ds(c * block, block)

    def cols(ch):
        return pl.ds(ch * cw, cw)

    last = slabs - 1
    later = last * ((s + ns - 1) // ns)

    def fresh_slot(c):
        return c if c == 0 else c + later

    def z_copy(src_ref, slot, ch, k):
        return pltpu.make_async_remote_copy(
            src_ref=src_ref,
            dst_ref=src.at[slot, rows(k + 1), cols(ch)],
            send_sem=zsend.at[slot, ch, k],
            recv_sem=zrecv.at[slot, ch, k],
            device_id=at(s, lax.rem(p - PEER_OFFSETS[k] + nd, nd)),
            device_id_type=MESH,
        )

    def x_copy(c, ch):
        return pltpu.make_async_remote_copy(
            src_ref=stage.at[c, :, cols(ch)],
            dst_ref=src.at[0 if c == 0 else c + last, rows(0), cols(ch)],
            send_sem=xsend.at[c, ch],
            recv_sem=xrecv.at[c, ch],
            device_id=at(lax.rem(s + 1, ns), p),
            device_id_type=MESH,
        )

    def given(j, ch):
        return stacked.at[rows(j), cols(ch)]

    def own(slot, ch):
        return src.at[slot, rows(0), cols(ch)]

    tile = lax.broadcasted_iota(jnp.int32, (block, edges.shape[1]), 1) // block
    degree = []
    for c in range(slabs):
        entries = edges[rows(c), :].astype(jnp.float32)
        total = jnp.ones((block, 1), jnp.float32)
        for j in range(slabs):
            scale = jnp.full(entries.shape, 1.0 if c == j else 0.0, jnp.float32)
            for k in range(len(PEER_OFFSETS)):
                wanted = jnp.where(picks[c, k] == j, 1.0, 0.0)
                scale = jnp.where(tile == k + 1, wanted, scale)
            masked = entries * scale
            masks[c, j] = masked.astype(jnp.bfloat16)
            total = total + jnp.sum(masked, axis=1, keepdims=True)
        degree.append(total)
    for j in range(1, slabs):
        src[j, rows(0), :] = stacked[rows(j), :]

    @pl.when(s == 0)
    def _():
        src[0, rows(0), :] = stacked[rows(0), :]

    pl.semaphore_wait(barrier, len(greeted))

    for ch in range(nch):
        @pl.when(s == 0)
        def _():
            for k in range(len(PEER_OFFSETS)):
                z_copy(given(0, ch), 0, ch, k).start()
        for j in range(1, slabs):
            for k in range(len(PEER_OFFSETS)):
                z_copy(given(j, ch), j, ch, k).start()

    def gather(c, j, slot, ch):
        return jnp.dot(
            masks[c, j], src[slot, :, cols(ch)], preferred_element_type=jnp.float32
        )

    def z_wait(slot, ch):
        for k in range(len(PEER_OFFSETS)):
            z_copy(own(slot, ch), slot, ch, k).wait_recv()

    w_self.wait()

    for c in range(slabs):
        slot = fresh_slot(c)
        for ch in range(nch):
            @pl.when(s > 0)
            def _():
                x_copy(c, ch).wait_recv()
                for k in range(len(PEER_OFFSETS)):
                    z_copy(own(slot, ch), slot, ch, k).start()
        for ch in range(nch):
            part = jnp.dot(
                src[slot, rows(0), cols(ch)], ws[cols(ch), :],
                preferred_element_type=jnp.float32,
            )
            if ch == 0:
                acc[...] = part
            else:
                acc[...] += part
        if c == 0:
            w_neigh.wait()
        for ch in range(nch):
            if c == 0:
                for j in range(1, slabs):
                    z_wait(j, ch)
            part = None
            for j in range(slabs):
                if j != c:
                    term = gather(c, j, fresh_slot(j) if j < c else j, ch)
                    part = term if part is None else part + term
            pre[:, cols(ch)] = part
        for ch in range(nch):
            if c == 0:
                z_wait(slot, ch)
            else:
                @pl.when(s > 0)
                def _():
                    z_wait(slot, ch)
            summed = pre[:, cols(ch)] + gather(c, c, slot, ch)
            mean = (summed / degree[c]).astype(jnp.bfloat16)
            if ch < nch - 1:
                acc[...] += jnp.dot(mean, wn[cols(ch), :], preferred_element_type=jnp.float32)
            else:
                for n in range(nch):
                    hidden = acc[:, cols(n)] + jnp.dot(
                        mean, wn[cols(ch), cols(n)], preferred_element_type=jnp.float32
                    )
                    stage[c, :, cols(n)] = jnp.maximum(hidden, 0.0).astype(jnp.bfloat16)

                    @pl.when(s < ns - 1)
                    def _():
                        x_copy(c, n).start()
        out[rows(c), :] = stage[c]

    for ch in range(nch):
        for k in range(len(PEER_OFFSETS)):
            for slot in range(slabs):
                z_copy(own(slot, ch), slot, ch, k).wait_send()
            for c in range(1, slabs):
                @pl.when(s > 0)
                def _():
                    z_copy(own(c + last, ch), c + last, ch, k).wait_send()
        for c in range(slabs):
            @pl.when(s < ns - 1)
            def _():
                x_copy(c, ch).wait_send()


def per_device(ns, nd, stacked, edges, picks, self_w, neigh_w):
    _, node_rows, width = stacked.shape
    tiles = len(PEER_OFFSETS) + 1
    block = edges.shape[1] // tiles
    slabs = node_rows // block
    nch = max(1, width // 256)
    slots = 2 * slabs - 1
    vmem = pl.BlockSpec(memory_space=pltpu.VMEM)
    hbm = pl.BlockSpec(memory_space=pl.ANY)
    result = pl.pallas_call(
        functools.partial(kernel, ns, nd, slabs, nch),
        out_shape=jax.ShapeDtypeStruct((node_rows, width), jnp.bfloat16),
        in_specs=[vmem, vmem, pl.BlockSpec(memory_space=pltpu.SMEM), hbm, hbm],
        out_specs=vmem,
        scratch_shapes=[
            pltpu.VMEM((width, width), jnp.bfloat16),
            pltpu.VMEM((width, width), jnp.bfloat16),
            pltpu.VMEM((slots, tiles * block, width), jnp.bfloat16),
            pltpu.VMEM((slabs, slabs, block, tiles * block), jnp.bfloat16),
            pltpu.VMEM((block, width), jnp.float32),
            pltpu.VMEM((block, width), jnp.float32),
            pltpu.VMEM((slabs, block, width), jnp.bfloat16),
            pltpu.SemaphoreType.DMA((2,)),
            pltpu.SemaphoreType.DMA((slots, nch, tiles - 1)),
            pltpu.SemaphoreType.DMA((slots, nch, tiles - 1)),
            pltpu.SemaphoreType.DMA((slabs, nch)),
            pltpu.SemaphoreType.DMA((slabs, nch)),
        ],
        compiler_params=pltpu.CompilerParams(collective_id=0, has_side_effects=True),
    )(stacked[0], edges, picks, self_w[0], neigh_w[0])
    return result[None]


def solution(mesh):
    in_specs = (
        P("section", "dom", None),
        P("dom", None),
        P("dom", None),
        P("section", None, None),
        P("section", None, None),
    )
    out_specs = P("section", "dom", None)
    ns, nd = mesh.shape["section"], mesh.shape["dom"]
    return jax.shard_map(
        functools.partial(per_device, ns, nd),
        mesh=mesh, in_specs=in_specs, out_specs=out_specs, check_vma=False,
    )
```

time: 152 us -> 58.5 us (0.38)
  the two profiles are of different devices: /device:TPU:4 before, /device:TPU:6 now
where the time goes in v1:
time: 58.5 us; the launch traced here: 58.4 us
  Pallas kernels  56.7 us (97%)
  local copies, waits for them, and re-layouts  1.67 us (3%)
    pallas_call x1, Pallas kernels, per_device(): pl.pallas_call(functools.partial(kernel, ns, nd, slabs, nch), out_shape=j...  56.7 us
    unnamed x1, local copies, waits for them, and re-layouts  1.67 us

profile of v1, /device:TPU:6, one launch (start us, length us, event | category | flops | bytes accessed | tf_op | source)
XLA Modules:
  0.0 58.4 jit_solution(8040084047523524416)
XLA Ops:
  0.0 56.7 %shard_map.55 = bf16[128,1024]{1,0:T(8,128)(2,1)} custom-call(bf16[128,1024]{1,0:T(8,128)(2,1)} %bitcast.7, s32[128,256]{1,0:T(8,128)} %edges.1, s32[2,3]{1,0:T(2,128)} %picks.1, bf16[1024,1024]{1,0:T(8,128)(2,1)} %bitcast.4, bf16[1024,1024]{1,0:T(8,128)(2,1)} %bitcast.5), custom_call_target="tpu_custom_call" | custom-call | tf_op jit(solution)/shard_map/pallas_call | solution.py:196
  56.7 1.7 %copy.7 = bf16[1,128,1024]{2,1,0:T(8,128)(2,1)} copy(bf16[1,128,1024]{2,1,0:T(8,128)(2,1)} %bitcast.6) | data formatting | bytes 524288

commit v2 on v1

--- a/solution.py
+++ b/solution.py
@@ -49,15 +49,38 @@
     def fresh_slot(c):
         return c if c == 0 else c + later
 
+    even = lax.rem(p, 2) == 0
+    partner = p + 1 - 2 * lax.rem(p, 2)
+    far = len(PEER_OFFSETS) - 1
+
     def z_copy(src_ref, slot, ch, k):
         return pltpu.make_async_remote_copy(
             src_ref=src_ref,
             dst_ref=src.at[slot, rows(k + 1), cols(ch)],
             send_sem=zsend.at[slot, ch, k],
             recv_sem=zrecv.at[slot, ch, k],
-            device_id=at(s, lax.rem(p - PEER_OFFSETS[k] + nd, nd)),
+            device_id=at(s, partner if k == 1 else lax.rem(p - PEER_OFFSETS[k] + nd, nd)),
             device_id_type=MESH,
         )
+
+    def z_send(src_ref, slot, ch):
+        z_copy(src_ref, slot, ch, 2).start()
+        z_copy(src_ref, slot, ch, 0).start()
+
+        @pl.when(jnp.logical_not(even))
+        def _():
+            z_copy(src_ref, slot, ch, 1).start()
+
+    def relay(slot, ch):
+        z_copy(own(slot, ch), slot, ch, 2).wait_recv()
+
+        @pl.when(even)
+        def _():
+            z_copy(src.at[slot, rows(far + 1), cols(ch)], slot, ch, 1).start()
+
+    def z_wait(slot, ch):
+        for k in (0, 1):
+            z_copy(own(slot, ch), slot, ch, k).wait_recv()
 
     def x_copy(c, ch):
         return pltpu.make_async_remote_copy(
@@ -101,31 +124,16 @@
     for ch in range(nch):
         @pl.when(s == 0)
         def _():
-            for k in range(len(PEER_OFFSETS)):
-                z_copy(given(0, ch), 0, ch, k).start()
+            z_send(given(0, ch), 0, ch)
         for j in range(1, slabs):
-            for k in range(len(PEER_OFFSETS)):
-                z_copy(given(j, ch), j, ch, k).start()
+            z_send(given(j, ch), j, ch)
 
     def gather(c, j, slot, ch):
         return jnp.dot(
             masks[c, j], src[slot, :, cols(ch)], preferred_element_type=jnp.float32
         )
 
-    def z_wait(slot, ch):
-        for k in range(len(PEER_OFFSETS)):
-            z_copy(own(slot, ch), slot, ch, k).wait_recv()
-
-    w_self.wait()
-
-    for c in range(slabs):
-        slot = fresh_slot(c)
-        for ch in range(nch):
-            @pl.when(s > 0)
-            def _():
-                x_copy(c, ch).wait_recv()
-                for k in range(len(PEER_OFFSETS)):
-                    z_copy(own(slot, ch), slot, ch, k).start()
+    def self_part(slot):
         for ch in range(nch):
             part = jnp.dot(
                 src[slot, rows(0), cols(ch)], ws[cols(ch), :],
@@ -135,8 +143,42 @@
                 acc[...] = part
             else:
                 acc[...] += part
+
+    def forward(c, ch):
+        x_copy(c, ch).wait_recv()
+        z_send(own(fresh_slot(c), ch), fresh_slot(c), ch)
+
+    w_self.wait()
+
+    @pl.when(s == 0)
+    def _():
+        self_part(0)
+
+    for ch in range(nch):
+        @pl.when(s == 0)
+        def _():
+            relay(0, ch)
+        for j in range(1, slabs):
+            relay(j, ch)
+
+    w_neigh.wait()
+
+    early = nch // 2
+    for c in range(slabs):
+        slot = fresh_slot(c)
         if c == 0:
-            w_neigh.wait()
+            @pl.when(s > 0)
+            def _():
+                for ch in range(nch):
+                    forward(0, ch)
+                self_part(0)
+        else:
+            @pl.when(s > 1)
+            def _():
+                for ch in range(early, nch):
+                    forward(c, ch)
+
+            self_part(slot)
         for ch in range(nch):
             if c == 0:
                 for j in range(1, slabs):
@@ -147,12 +189,29 @@
                     term = gather(c, j, fresh_slot(j) if j < c else j, ch)
                     part = term if part is None else part + term
             pre[:, cols(ch)] = part
+
+        @pl.when(s > 0)
+        def _():
+            relay(slot, 0)
         for ch in range(nch):
+            if ch == nch - 1 and c + 1 < slabs:
+                @pl.when(s == 1)
+                def _():
+                    for n in range(nch):
+                        forward(c + 1, n)
+
+                @pl.when(s > 1)
+                def _():
+                    for n in range(early):
+                        forward(c + 1, n)
             if c == 0:
                 z_wait(slot, ch)
-            else:
-                @pl.when(s > 0)
-                def _():
+
+            @pl.when(s > 0)
+            def _():
+                if ch < nch - 1:
+                    relay(slot, ch + 1)
+                if c > 0:
                     z_wait(slot, ch)
             summed = pre[:, cols(ch)] + gather(c, c, slot, ch)
             mean = (summed / degree[c]).astype(jnp.bfloat16)

time: 58.5 us -> 57.9 us (0.990)
  Pallas kernels: 56.7 us -> 56 us
    pallas_call x1, Pallas kernels: 56.7 us -> 56 us  [per_device(): pl.pallas_call(functools.partial(kernel, ns, nd, slabs, nch), out_shape=j...]
where the time goes in v2:
time: 57.9 us; the launch traced here: 57.7 us
  Pallas kernels  56 us (97%)
  local copies, waits for them, and re-layouts  1.67 us (3%)
    pallas_call x1, Pallas kernels, per_device(): pl.pallas_call(functools.partial(kernel, ns, nd, slabs, nch), out_shape=j...  56 us
    unnamed x1, local copies, waits for them, and re-layouts  1.67 us

profile of v2, /device:TPU:6, one launch (start us, length us, event | category | flops | bytes accessed | tf_op | source)
XLA Modules:
  0.0 57.7 jit_solution(1424242478431302109)
XLA Ops:
  0.0 56.0 %shard_map.55 = bf16[128,1024]{1,0:T(8,128)(2,1)} custom-call(bf16[128,1024]{1,0:T(8,128)(2,1)} %bitcast.7, s32[128,256]{1,0:T(8,128)} %edges.1, s32[2,3]{1,0:T(2,128)} %picks.1, bf16[1024,1024]{1,0:T(8,128)(2,1)} %bitcast.4, bf16[1024,1024]{1,0:T(8,128)(2,1)} %bitcast.5), custom_call_target="tpu_custom_call" | custom-call | tf_op jit(solution)/shard_map/pallas_call | solution.py:255
  56.0 1.7 %copy.7 = bf16[1,128,1024]{2,1,0:T(8,128)(2,1)} copy(bf16[1,128,1024]{2,1,0:T(8,128)(2,1)} %bitcast.6) | data formatting | bytes 524288

commit v3 on v2

--- a/solution.py
+++ b/solution.py
@@ -14,8 +14,8 @@
 def kernel(
     ns, nd, slabs, nch,
     stacked, edges, picks, ws_hbm, wn_hbm, out,
-    ws, wn, src, masks, pre, acc, stage,
-    wsem, zsend, zrecv, xsend, xrecv,
+    ws, wn, src, masks, pre, acc, stage, above, sums, summed_below,
+    wsem, zsend, zrecv, xsend, xrecv, psend, precv,
 ):
     block = edges.shape[1] // (len(PEER_OFFSETS) + 1)
     width = stacked.shape[1]
@@ -44,10 +44,6 @@
         return pl.ds(ch * cw, cw)
 
     last = slabs - 1
-    later = last * ((s + ns - 1) // ns)
-
-    def fresh_slot(c):
-        return c if c == 0 else c + later
 
     even = lax.rem(p, 2) == 0
     partner = p + 1 - 2 * lax.rem(p, 2)
@@ -59,7 +55,7 @@
             dst_ref=src.at[slot, rows(k + 1), cols(ch)],
             send_sem=zsend.at[slot, ch, k],
             recv_sem=zrecv.at[slot, ch, k],
-            device_id=at(s, partner if k == 1 else lax.rem(p - PEER_OFFSETS[k] + nd, nd)),
+            device_id=at(s, partner if k == 1 and ch < nch - 1 else lax.rem(p - PEER_OFFSETS[k] + nd, nd)),
             device_id_type=MESH,
         )
 
@@ -67,16 +63,20 @@
         z_copy(src_ref, slot, ch, 2).start()
         z_copy(src_ref, slot, ch, 0).start()
 
-        @pl.when(jnp.logical_not(even))
-        def _():
+        if ch == nch - 1:
             z_copy(src_ref, slot, ch, 1).start()
+        else:
+            @pl.when(jnp.logical_not(even))
+            def _():
+                z_copy(src_ref, slot, ch, 1).start()
 
     def relay(slot, ch):
         z_copy(own(slot, ch), slot, ch, 2).wait_recv()
 
-        @pl.when(even)
-        def _():
-            z_copy(src.at[slot, rows(far + 1), cols(ch)], slot, ch, 1).start()
+        if ch < nch - 1:
+            @pl.when(even)
+            def _():
+                z_copy(src.at[slot, rows(far + 1), cols(ch)], slot, ch, 1).start()
 
     def z_wait(slot, ch):
         for k in (0, 1):
@@ -85,9 +85,19 @@
     def x_copy(c, ch):
         return pltpu.make_async_remote_copy(
             src_ref=stage.at[c, :, cols(ch)],
-            dst_ref=src.at[0 if c == 0 else c + last, rows(0), cols(ch)],
+            dst_ref=src.at[0, rows(0), cols(ch)] if c == 0 else above.at[c - 1, :, cols(ch)],
             send_sem=xsend.at[c, ch],
             recv_sem=xrecv.at[c, ch],
+            device_id=at(lax.rem(s + 1, ns), p),
+            device_id_type=MESH,
+        )
+
+    def sum_copy(c, ch):
+        return pltpu.make_async_remote_copy(
+            src_ref=sums.at[c - 1, :, cols(ch)],
+            dst_ref=summed_below.at[c - 1, :, cols(ch)],
+            send_sem=psend.at[c - 1, ch],
+            recv_sem=precv.at[c - 1, ch],
             device_id=at(lax.rem(s + 1, ns), p),
             device_id_type=MESH,
         )
@@ -133,26 +143,21 @@
             masks[c, j], src[slot, :, cols(ch)], preferred_element_type=jnp.float32
         )
 
-    def self_part(slot):
+    def self_part(ref):
         for ch in range(nch):
             part = jnp.dot(
-                src[slot, rows(0), cols(ch)], ws[cols(ch), :],
-                preferred_element_type=jnp.float32,
+                ref[:, cols(ch)], ws[cols(ch), :], preferred_element_type=jnp.float32
             )
             if ch == 0:
                 acc[...] = part
             else:
                 acc[...] += part
 
-    def forward(c, ch):
-        x_copy(c, ch).wait_recv()
-        z_send(own(fresh_slot(c), ch), fresh_slot(c), ch)
-
     w_self.wait()
 
     @pl.when(s == 0)
     def _():
-        self_part(0)
+        self_part(src.at[0, rows(0)])
 
     for ch in range(nch):
         @pl.when(s == 0)
@@ -163,84 +168,112 @@
 
     w_neigh.wait()
 
-    early = nch // 2
-    for c in range(slabs):
-        slot = fresh_slot(c)
-        if c == 0:
+    def produce(c, n, mean):
+        hidden = acc[:, cols(n)] + jnp.dot(
+            mean, wn[cols(nch - 1), cols(n)], preferred_element_type=jnp.float32
+        )
+        made = jnp.maximum(hidden, 0.0).astype(jnp.bfloat16)
+        stage[c, :, cols(n)] = made
+        out[rows(c), cols(n)] = made
+        if c > 0:
+            src[c + last, rows(0), cols(n)] = made
+
+        @pl.when(s < ns - 1)
+        def _():
+            if c > 0:
+                z_send(own(c + last, n), c + last, n)
+            x_copy(c, n).start()
+
+    def finish(c, ch, summed):
+        mean = (summed / degree[c]).astype(jnp.bfloat16)
+        if ch < nch - 1:
+            acc[...] += jnp.dot(mean, wn[cols(ch), :], preferred_element_type=jnp.float32)
+        else:
+            for n in range(nch):
+                produce(c, n, mean)
+
+    @pl.when(s > 0)
+    def _():
+        for ch in range(nch):
+            x_copy(0, ch).wait_recv()
+            z_send(own(0, ch), 0, ch)
+        self_part(src.at[0, rows(0)])
+
+    for ch in range(nch):
+        part = None
+        for j in range(1, slabs):
+            z_wait(j, ch)
+            term = gather(0, j, j, ch)
+            part = term if part is None else part + term
+        pre[:, cols(ch)] = jnp.zeros((block, cw), jnp.float32) if part is None else part
+
+    @pl.when(s > 0)
+    def _():
+        relay(0, 0)
+    for ch in range(nch):
+        z_wait(0, ch)
+        if ch < nch - 1:
             @pl.when(s > 0)
             def _():
-                for ch in range(nch):
-                    forward(0, ch)
-                self_part(0)
-        else:
-            @pl.when(s > 1)
-            def _():
-                for ch in range(early, nch):
-                    forward(c, ch)
-
-            self_part(slot)
+                relay(0, ch + 1)
+        finish(0, ch, pre[:, cols(ch)] + gather(0, 0, 0, ch))
+
+    for c in range(1, slabs):
         for ch in range(nch):
-            if c == 0:
-                for j in range(1, slabs):
-                    z_wait(j, ch)
-            part = None
-            for j in range(slabs):
-                if j != c:
-                    term = gather(c, j, fresh_slot(j) if j < c else j, ch)
-                    part = term if part is None else part + term
+            part = gather(c, 0, 0, ch)
+            for j in range(c + 1, slabs):
+                part = part + gather(c, j, j, ch)
             pre[:, cols(ch)] = part
 
+        @pl.when(s == 0)
+        def _():
+            self_part(src.at[c, rows(0)])
+            for ch in range(nch):
+                part = pre[:, cols(ch)]
+                for j in range(1, c + 1):
+                    part = part + gather(c, j, j, ch)
+                pre[:, cols(ch)] = part
+
         @pl.when(s > 0)
         def _():
-            relay(slot, 0)
+            for ch in range(nch):
+                x_copy(c, ch).wait_recv()
+            self_part(above.at[c - 1])
+
         for ch in range(nch):
-            if ch == nch - 1 and c + 1 < slabs:
-                @pl.when(s == 1)
-                def _():
-                    for n in range(nch):
-                        forward(c + 1, n)
-
-                @pl.when(s > 1)
-                def _():
-                    for n in range(early):
-                        forward(c + 1, n)
-            if c == 0:
-                z_wait(slot, ch)
-
             @pl.when(s > 0)
             def _():
+                sum_copy(c, ch).wait_recv()
+                pre[:, cols(ch)] += summed_below[c - 1, :, cols(ch)].astype(jnp.float32)
+            finish(c, ch, pre[:, cols(ch)])
+
+        @pl.when(s < ns - 1)
+        def _():
+            relay(c + last, 0)
+            for ch in range(nch):
                 if ch < nch - 1:
-                    relay(slot, ch + 1)
-                if c > 0:
-                    z_wait(slot, ch)
-            summed = pre[:, cols(ch)] + gather(c, c, slot, ch)
-            mean = (summed / degree[c]).astype(jnp.bfloat16)
-            if ch < nch - 1:
-                acc[...] += jnp.dot(mean, wn[cols(ch), :], preferred_element_type=jnp.float32)
-            else:
-                for n in range(nch):
-                    hidden = acc[:, cols(n)] + jnp.dot(
-                        mean, wn[cols(ch), cols(n)], preferred_element_type=jnp.float32
-                    )
-                    stage[c, :, cols(n)] = jnp.maximum(hidden, 0.0).astype(jnp.bfloat16)
-
-                    @pl.when(s < ns - 1)
-                    def _():
-                        x_copy(c, n).start()
-        out[rows(c), :] = stage[c]
+                    relay(c + last, ch + 1)
+                z_wait(c + last, ch)
+                part = None
+                for j in range(1, c + 1):
+                    term = gather(c, j, j + last, ch)
+                    part = term if part is None else part + term
+                sums[c - 1, :, cols(ch)] = part.astype(jnp.bfloat16)
+                sum_copy(c, ch).start()
 
     for ch in range(nch):
         for k in range(len(PEER_OFFSETS)):
             for slot in range(slabs):
                 z_copy(own(slot, ch), slot, ch, k).wait_send()
+
+        @pl.when(s < ns - 1)
+        def _():
+            for c in range(slabs):
+                x_copy(c, ch).wait_send()
             for c in range(1, slabs):
-                @pl.when(s > 0)
-                def _():
+                sum_copy(c, ch).wait_send()
+                for k in range(len(PEER_OFFSETS)):
                     z_copy(own(c + last, ch), c + last, ch, k).wait_send()
-        for c in range(slabs):
-            @pl.when(s < ns - 1)
-            def _():
-                x_copy(c, ch).wait_send()
 
 
 def per_device(ns, nd, stacked, edges, picks, self_w, neigh_w):
@@ -250,6 +283,7 @@
     slabs = node_rows // block
     nch = max(1, width // 256)
     slots = 2 * slabs - 1
+    others = max(1, slabs - 1)
     vmem = pl.BlockSpec(memory_space=pltpu.VMEM)
     hbm = pl.BlockSpec(memory_space=pl.ANY)
     result = pl.pallas_call(
@@ -265,11 +299,16 @@
             pltpu.VMEM((block, width), jnp.float32),
             pltpu.VMEM((block, width), jnp.float32),
             pltpu.VMEM((slabs, block, width), jnp.bfloat16),
+            pltpu.VMEM((others, block, width), jnp.bfloat16),
+            pltpu.VMEM((others, block, width), jnp.bfloat16),
+            pltpu.VMEM((others, block, width), jnp.bfloat16),
             pltpu.SemaphoreType.DMA((2,)),
             pltpu.SemaphoreType.DMA((slots, nch, tiles - 1)),
             pltpu.SemaphoreType.DMA((slots, nch, tiles - 1)),
             pltpu.SemaphoreType.DMA((slabs, nch)),
             pltpu.SemaphoreType.DMA((slabs, nch)),
+            pltpu.SemaphoreType.DMA((others, nch)),
+            pltpu.SemaphoreType.DMA((others, nch)),
         ],
         compiler_params=pltpu.CompilerParams(collective_id=0, has_side_effects=True),
     )(stacked[0], edges, picks, self_w[0], neigh_w[0])

time: 57.9 us -> 53.1 us (0.917)
  Pallas kernels: 56 us -> 51.3 us
    pallas_call x1, Pallas kernels: 56 us -> 51.3 us  [per_device(): pl.pallas_call(functools.partial(kernel, ns, nd, slabs, nch), out_shape=j...]
where the time goes in v3:
time: 53.1 us; the launch traced here: 52.9 us
  Pallas kernels  51.3 us (97%)
  local copies, waits for them, and re-layouts  1.67 us (3%)
    pallas_call x1, Pallas kernels, per_device(): pl.pallas_call(functools.partial(kernel, ns, nd, slabs, nch), out_shape=j...  51.3 us
    unnamed x1, local copies, waits for them, and re-layouts  1.67 us

profile of v3, /device:TPU:6, one launch (start us, length us, event | category | flops | bytes accessed | tf_op | source)
XLA Modules:
  0.0 52.9 jit_solution(14722663568270813544)
XLA Ops:
  0.0 51.3 %shard_map.55 = bf16[128,1024]{1,0:T(8,128)(2,1)} custom-call(bf16[128,1024]{1,0:T(8,128)(2,1)} %bitcast.7, s32[128,256]{1,0:T(8,128)} %edges.1, s32[2,3]{1,0:T(2,128)} %picks.1, bf16[1024,1024]{1,0:T(8,128)(2,1)} %bitcast.4, bf16[1024,1024]{1,0:T(8,128)(2,1)} %bitcast.5), custom_call_target="tpu_custom_call" | custom-call | tf_op jit(solution)/shard_map/pallas_call | solution.py:289
  51.3 1.7 %copy.7 = bf16[1,128,1024]{2,1,0:T(8,128)(2,1)} copy(bf16[1,128,1024]{2,1,0:T(8,128)(2,1)} %bitcast.6) | data formatting | bytes 524288

commit v4 on v3

--- a/solution.py
+++ b/solution.py
@@ -55,28 +55,24 @@
             dst_ref=src.at[slot, rows(k + 1), cols(ch)],
             send_sem=zsend.at[slot, ch, k],
             recv_sem=zrecv.at[slot, ch, k],
-            device_id=at(s, partner if k == 1 and ch < nch - 1 else lax.rem(p - PEER_OFFSETS[k] + nd, nd)),
+            device_id=at(s, partner if k == 1 else lax.rem(p - PEER_OFFSETS[k] + nd, nd)),
             device_id_type=MESH,
         )
 
     def z_send(src_ref, slot, ch):
+        z_copy(src_ref, slot, ch, 0).start()
         z_copy(src_ref, slot, ch, 2).start()
-        z_copy(src_ref, slot, ch, 0).start()
-
-        if ch == nch - 1:
+
+        @pl.when(jnp.logical_not(even))
+        def _():
             z_copy(src_ref, slot, ch, 1).start()
-        else:
-            @pl.when(jnp.logical_not(even))
-            def _():
-                z_copy(src_ref, slot, ch, 1).start()
 
     def relay(slot, ch):
         z_copy(own(slot, ch), slot, ch, 2).wait_recv()
 
-        if ch < nch - 1:
-            @pl.when(even)
-            def _():
-                z_copy(src.at[slot, rows(far + 1), cols(ch)], slot, ch, 1).start()
+        @pl.when(even)
+        def _():
+            z_copy(src.at[slot, rows(far + 1), cols(ch)], slot, ch, 1).start()
 
     def z_wait(slot, ch):
         for k in (0, 1):

time: 53.1 us -> 52 us (0.979)
  Pallas kernels: 51.3 us -> 49.8 us
    pallas_call x1, Pallas kernels: 51.3 us -> 49.8 us  [per_device(): pl.pallas_call(functools.partial(kernel, ns, nd, slabs, nch), out_shape=j...]
where the time goes in v4:
time: 52 us; the launch traced here: 51.5 us
  Pallas kernels  49.8 us (96%)
  local copies, waits for them, and re-layouts  1.67 us (3%)
    pallas_call x1, Pallas kernels, per_device(): pl.pallas_call(functools.partial(kernel, ns, nd, slabs, nch), out_shape=j...  49.8 us
    unnamed x1, local copies, waits for them, and re-layouts  1.67 us

profile of v4, /device:TPU:6, one launch (start us, length us, event | category | flops | bytes accessed | tf_op | source)
XLA Modules:
  0.0 51.5 jit_solution(5332416431768162893)
XLA Ops:
  0.0 49.8 %shard_map.55 = bf16[128,1024]{1,0:T(8,128)(2,1)} custom-call(bf16[128,1024]{1,0:T(8,128)(2,1)} %bitcast.7, s32[128,256]{1,0:T(8,128)} %edges.1, s32[2,3]{1,0:T(2,128)} %picks.1, bf16[1024,1024]{1,0:T(8,128)(2,1)} %bitcast.4, bf16[1024,1024]{1,0:T(8,128)(2,1)} %bitcast.5), custom_call_target="tpu_custom_call" | custom-call | tf_op jit(solution)/shard_map/pallas_call | solution.py:285
  49.8 1.7 %copy.7 = bf16[1,128,1024]{2,1,0:T(8,128)(2,1)} copy(bf16[1,128,1024]{2,1,0:T(8,128)(2,1)} %bitcast.6) | data formatting | bytes 524288

commit v5 on v4

--- a/solution.py
+++ b/solution.py
@@ -15,7 +15,9 @@
     ns, nd, slabs, nch,
     stacked, edges, picks, ws_hbm, wn_hbm, out,
     ws, wn, src, masks, pre, acc, stage, above, sums, summed_below,
+    lent, lent_mean, aided_mean, mean_now,
     wsem, zsend, zrecv, xsend, xrecv, psend, precv,
+    lsend, lrecv, msend, mrecv, lzsend, lzrecv,
 ):
     block = edges.shape[1] // (len(PEER_OFFSETS) + 1)
     width = stacked.shape[1]
@@ -97,9 +99,6 @@
             device_id=at(lax.rem(s + 1, ns), p),
             device_id_type=MESH,
         )
-
-    def given(j, ch):
-        return stacked.at[rows(j), cols(ch)]
 
     def own(slot, ch):
         return src.at[slot, rows(0), cols(ch)]
@@ -127,12 +126,66 @@
 
     pl.semaphore_wait(barrier, len(greeted))
 
+    aided = nch - 1
+
+    def lend_copy(j):
+        return pltpu.make_async_remote_copy(
+            src_ref=own(j, aided),
+            dst_ref=lent.at[j, rows(0)],
+            send_sem=lsend.at[j],
+            recv_sem=lrecv.at[j],
+            device_id=at(lax.rem(s + 1, ns), p),
+            device_id_type=MESH,
+        )
+
+    def lent_copy(src_row, j, k):
+        return pltpu.make_async_remote_copy(
+            src_ref=lent.at[j, rows(src_row)],
+            dst_ref=lent.at[j, rows(k + 1)],
+            send_sem=lzsend.at[j, k],
+            recv_sem=lzrecv.at[j, k],
+            device_id=at(s, partner if k == 1 else lax.rem(p - PEER_OFFSETS[k] + nd, nd)),
+            device_id_type=MESH,
+        )
+
+    def mean_copy(c):
+        return pltpu.make_async_remote_copy(
+            src_ref=lent_mean.at[c],
+            dst_ref=aided_mean.at[c],
+            send_sem=msend.at[c],
+            recv_sem=mrecv.at[c],
+            device_id=at(lax.rem(s + ns - 1, ns), p),
+            device_id_type=MESH,
+        )
+
+    @pl.when(s == 0)
+    def _():
+        for j in range(slabs):
+            lend_copy(j).start()
+
+    @pl.when(s == 1)
+    def _():
+        for j in range(slabs):
+            lend_copy(j).wait_recv()
+            lent_copy(0, j, 0).start()
+            lent_copy(0, j, 2).start()
+
+            @pl.when(jnp.logical_not(even))
+            def _():
+                lent_copy(0, j, 1).start()
+
     for ch in range(nch):
-        @pl.when(s == 0)
-        def _():
-            z_send(given(0, ch), 0, ch)
-        for j in range(1, slabs):
-            z_send(given(j, ch), j, ch)
+        if ch != aided:
+            @pl.when(s == 0)
+            def _():
+                z_send(own(0, ch), 0, ch)
+            for j in range(1, slabs):
+                z_send(own(j, ch), j, ch)
+        else:
+            @pl.when(s > 0)
+            def _():
+                for j in range(1, slabs):
+                    z_send(own(j, ch), j, ch)
 
     def gather(c, j, slot, ch):
         return jnp.dot(
@@ -155,12 +208,37 @@
     def _():
         self_part(src.at[0, rows(0)])
 
+    @pl.when(s == 1)
+    def _():
+        for j in range(slabs):
+            lent_copy(0, j, 2).wait_recv()
+
+            @pl.when(even)
+            def _():
+                lent_copy(far + 1, j, 1).start()
+        for j in range(slabs):
+            for k in (0, 1):
+                lent_copy(0, j, k).wait_recv()
+        for c in range(slabs):
+            summed = None
+            for j in range(slabs):
+                term = jnp.dot(masks[c, j], lent[j], preferred_element_type=jnp.float32)
+                summed = term if summed is None else summed + term
+            lent_mean[c] = (summed / degree[c]).astype(jnp.bfloat16)
+            mean_copy(c).start()
+
     for ch in range(nch):
-        @pl.when(s == 0)
-        def _():
-            relay(0, ch)
-        for j in range(1, slabs):
-            relay(j, ch)
+        if ch != aided:
+            @pl.when(s == 0)
+            def _():
+                relay(0, ch)
+            for j in range(1, slabs):
+                relay(j, ch)
+        else:
+            @pl.when(s > 0)
+            def _():
+                for j in range(1, slabs):
+                    relay(j, ch)
 
     w_neigh.wait()
 
@@ -180,14 +258,22 @@
                 z_send(own(c + last, n), c + last, n)
             x_copy(c, n).start()
 
-    def finish(c, ch, summed):
-        mean = (summed / degree[c]).astype(jnp.bfloat16)
+    def finish(c, ch, mean):
         if ch < nch - 1:
             acc[...] += jnp.dot(mean, wn[cols(ch), :], preferred_element_type=jnp.float32)
         else:
             for n in range(nch):
                 produce(c, n, mean)
 
+    def mean_of(c, summed):
+        return (summed / degree[c]).astype(jnp.bfloat16)
+
+    def use_aid(c):
+        @pl.when(s == 0)
+        def _():
+            mean_copy(c).wait_recv()
+            mean_now[...] = aided_mean[c]
+
     @pl.when(s > 0)
     def _():
         for ch in range(nch):
@@ -195,36 +281,55 @@
             z_send(own(0, ch), 0, ch)
         self_part(src.at[0, rows(0)])
 
-    for ch in range(nch):
-        part = None
+    def history(ch):
+        part = jnp.zeros((block, cw), jnp.float32)
         for j in range(1, slabs):
             z_wait(j, ch)
-            term = gather(0, j, j, ch)
-            part = term if part is None else part + term
-        pre[:, cols(ch)] = jnp.zeros((block, cw), jnp.float32) if part is None else part
+            part = part + gather(0, j, j, ch)
+        pre[:, cols(ch)] = part
+
+    for ch in range(nch):
+        if ch != aided:
+            history(ch)
+        else:
+            pl.when(s > 0)(functools.partial(history, ch))
 
     @pl.when(s > 0)
     def _():
         relay(0, 0)
     for ch in range(nch):
-        z_wait(0, ch)
-        if ch < nch - 1:
+        if ch == aided:
             @pl.when(s > 0)
             def _():
+                z_wait(0, ch)
+                mean_now[...] = mean_of(0, pre[:, cols(ch)] + gather(0, 0, 0, ch))
+            use_aid(0)
+            finish(0, ch, mean_now[...])
+        else:
+            z_wait(0, ch)
+
+            @pl.when(s > 0)
+            def _():
                 relay(0, ch + 1)
-        finish(0, ch, pre[:, cols(ch)] + gather(0, 0, 0, ch))
+            finish(0, ch, mean_of(0, pre[:, cols(ch)] + gather(0, 0, 0, ch)))
 
     for c in range(1, slabs):
-        for ch in range(nch):
+        def present(ch):
             part = gather(c, 0, 0, ch)
             for j in range(c + 1, slabs):
                 part = part + gather(c, j, j, ch)
             pre[:, cols(ch)] = part
 
+        for ch in range(nch):
+            if ch != aided:
+                present(ch)
+            else:
+                pl.when(s > 0)(functools.partial(present, ch))
+
         @pl.when(s == 0)
         def _():
             self_part(src.at[c, rows(0)])
-            for ch in range(nch):
+            for ch in range(aided):
                 part = pre[:, cols(ch)]
                 for j in range(1, c + 1):
                     part = part + gather(c, j, j, ch)
@@ -241,7 +346,14 @@
             def _():
                 sum_copy(c, ch).wait_recv()
                 pre[:, cols(ch)] += summed_below[c - 1, :, cols(ch)].astype(jnp.float32)
-            finish(c, ch, pre[:, cols(ch)])
+            if ch == aided:
+                @pl.when(s > 0)
+                def _():
+                    mean_now[...] = mean_of(c, pre[:, cols(ch)])
+                use_aid(c)
+                finish(c, ch, mean_now[...])
+            else:
+                finish(c, ch, mean_of(c, pre[:, cols(ch)]))
 
         @pl.when(s < ns - 1)
         def _():
@@ -260,7 +372,10 @@
     for ch in range(nch):
         for k in range(len(PEER_OFFSETS)):
             for slot in range(slabs):
-                z_copy(own(slot, ch), slot, ch, k).wait_send()
+                if ch == aided:
+                    pl.when(s > 0)(z_copy(own(slot, ch), slot, ch, k).wait_send)
+                else:
+                    z_copy(own(slot, ch), slot, ch, k).wait_send()
 
         @pl.when(s < ns - 1)
         def _():
@@ -270,6 +385,19 @@
                 sum_copy(c, ch).wait_send()
                 for k in range(len(PEER_OFFSETS)):
                     z_copy(own(c + last, ch), c + last, ch, k).wait_send()
+
+
+    @pl.when(s == 0)
+    def _():
+        for j in range(slabs):
+            lend_copy(j).wait_send()
+
+    @pl.when(s == 1)
+    def _():
+        for j in range(slabs):
+            for k in range(len(PEER_OFFSETS)):
+                lent_copy(0, j, k).wait_send()
+            mean_copy(j).wait_send()
 
 
 def per_device(ns, nd, stacked, edges, picks, self_w, neigh_w):
@@ -298,6 +426,10 @@
             pltpu.VMEM((others, block, width), jnp.bfloat16),
             pltpu.VMEM((others, block, width), jnp.bfloat16),
             pltpu.VMEM((others, block, width), jnp.bfloat16),
+            pltpu.VMEM((slabs, tiles * block, width // nch), jnp.bfloat16),
+            pltpu.VMEM((slabs, block, width // nch), jnp.bfloat16),
+            pltpu.VMEM((slabs, block, width // nch), jnp.bfloat16),
+            pltpu.VMEM((block, width // nch), jnp.bfloat16),
             pltpu.SemaphoreType.DMA((2,)),
             pltpu.SemaphoreType.DMA((slots, nch, tiles - 1)),
             pltpu.SemaphoreType.DMA((slots, nch, tiles - 1)),
@@ -305,6 +437,12 @@
             pltpu.SemaphoreType.DMA((slabs, nch)),
             pltpu.SemaphoreType.DMA((others, nch)),
             pltpu.SemaphoreType.DMA((others, nch)),
+            pltpu.SemaphoreType.DMA((slabs,)),
+            pltpu.SemaphoreType.DMA((slabs,)),
+            pltpu.SemaphoreType.DMA((slabs,)),
+            pltpu.SemaphoreType.DMA((slabs,)),
+            pltpu.SemaphoreType.DMA((slabs, tiles - 1)),
+            pltpu.SemaphoreType.DMA((slabs, tiles - 1)),
         ],
         compiler_params=pltpu.CompilerParams(collective_id=0, has_side_effects=True),
     )(stacked[0], edges, picks, self_w[0], neigh_w[0])

time: 52 us -> 52.8 us (1.015)
  Pallas kernels: 49.8 us -> 50.6 us
    pallas_call x1, Pallas kernels: 49.8 us -> 50.6 us  [per_device(): pl.pallas_call(functools.partial(kernel, ns, nd, slabs, nch), out_shape=j...]
where the time goes in v5:
time: 52.8 us; the launch traced here: 52.2 us
  Pallas kernels  50.6 us (96%)
  local copies, waits for them, and re-layouts  1.67 us (3%)
    pallas_call x1, Pallas kernels, per_device(): pl.pallas_call(functools.partial(kernel, ns, nd, slabs, nch), out_shape=j...  50.6 us
    unnamed x1, local copies, waits for them, and re-layouts  1.67 us

profile of v5, /device:TPU:6, one launch (start us, length us, event | category | flops | bytes accessed | tf_op | source)
XLA Modules:
  0.0 52.2 jit_solution(7267006085162322640)
XLA Ops:
  0.0 50.6 %shard_map.55 = bf16[128,1024]{1,0:T(8,128)(2,1)} custom-call(bf16[128,1024]{1,0:T(8,128)(2,1)} %bitcast.7, s32[128,256]{1,0:T(8,128)} %edges.1, s32[2,3]{1,0:T(2,128)} %picks.1, bf16[1024,1024]{1,0:T(8,128)(2,1)} %bitcast.4, bf16[1024,1024]{1,0:T(8,128)(2,1)} %bitcast.5), custom_call_target="tpu_custom_call" | custom-call | tf_op jit(solution)/shard_map/pallas_call | solution.py:413
  50.6 1.7 %copy.7 = bf16[1,128,1024]{2,1,0:T(8,128)(2,1)} copy(bf16[1,128,1024]{2,1,0:T(8,128)(2,1)} %bitcast.6) | data formatting | bytes 524288

commit v6 on v4

--- a/solution.py
+++ b/solution.py
@@ -205,13 +205,10 @@
 
     @pl.when(s > 0)
     def _():
-        relay(0, 0)
+        for ch in range(nch):
+            relay(0, ch)
     for ch in range(nch):
         z_wait(0, ch)
-        if ch < nch - 1:
-            @pl.when(s > 0)
-            def _():
-                relay(0, ch + 1)
         finish(0, ch, pre[:, cols(ch)] + gather(0, 0, 0, ch))
 
     for c in range(1, slabs):
@@ -245,10 +242,9 @@
 
         @pl.when(s < ns - 1)
         def _():
-            relay(c + last, 0)
             for ch in range(nch):
-                if ch < nch - 1:
-                    relay(c + last, ch + 1)
+                relay(c + last, ch)
+            for ch in range(nch):
                 z_wait(c + last, ch)
                 part = None
                 for j in range(1, c + 1):

time: 52 us -> 53.8 us (1.035)
  Pallas kernels: 49.8 us -> 52 us
    pallas_call x1, Pallas kernels: 49.8 us -> 52 us  [per_device(): pl.pallas_call(functools.partial(kernel, ns, nd, slabs, nch), out_shape=j...]
where the time goes in v6:
time: 53.8 us; the launch traced here: 53.6 us
  Pallas kernels  52 us (97%)
  local copies, waits for them, and re-layouts  1.67 us (3%)
    pallas_call x1, Pallas kernels, per_device(): pl.pallas_call(functools.partial(kernel, ns, nd, slabs, nch), out_shape=j...  52 us
    unnamed x1, local copies, waits for them, and re-layouts  1.67 us

profile of v6, /device:TPU:6, one launch (start us, length us, event | category | flops | bytes accessed | tf_op | source)
XLA Modules:
  0.0 53.6 jit_solution(13993950369823756636)
XLA Ops:
  0.0 52.0 %shard_map.55 = bf16[128,1024]{1,0:T(8,128)(2,1)} custom-call(bf16[128,1024]{1,0:T(8,128)(2,1)} %bitcast.7, s32[128,256]{1,0:T(8,128)} %edges.1, s32[2,3]{1,0:T(2,128)} %picks.1, bf16[1024,1024]{1,0:T(8,128)(2,1)} %bitcast.4, bf16[1024,1024]{1,0:T(8,128)(2,1)} %bitcast.5), custom_call_target="tpu_custom_call" | custom-call | tf_op jit(solution)/shard_map/pallas_call | solution.py:281
  52.0 1.7 %copy.7 = bf16[1,128,1024]{2,1,0:T(8,128)(2,1)} copy(bf16[1,128,1024]{2,1,0:T(8,128)(2,1)} %bitcast.6) | data formatting | bytes 524288
